TPU v7x, 128 devices: a whole 4x4x4 slice. The times are simulated.
128 devices in a mesh: node: 32 (over x, y, core), local: 4 (over z).
Axes of the slice: x: 4, y: 4, z: 4, core: 2. Of those that a mesh axis runs over, the one named last changes fastest.
Arguments:
- tokens_in: bfloat16 [16384, 3584], P(('node', 'local')), may hold values from -6 to 6
- grad_out: bfloat16 [16384, 3584], P(('node', 'local')), may hold values from -6 to 6
- expert_ids: int32 [16384, 3], P(('node', 'local')), may hold values from 0 to 127, as said below
- gate_weights: float32 [16384, 3], P(('node', 'local')), may hold values from 0.2 to 1
- w_gate: bfloat16 [128, 3584, 1024], P(('node', 'local')), may hold values from -0.09375 to 0.09375
- w_up: bfloat16 [128, 3584, 1024], P(('node', 'local')), may hold values from -0.09375 to 0.09375
- w_down: bfloat16 [128, 1024, 3584], P(('node', 'local')), may hold values from -0.09375 to 0.09375
Outputs:
- grad_in: bfloat16 [16384, 3584], P(('node', 'local'))
Inputs may be any that keep to these rules, and one draw needn't show every extreme that they name: `expert_ids`: each row names 3 different experts. Among the 128 tokens of one device no expert is named more than 6 times, and one expert is named exactly 6 times by the tokens of every device.
All inputs are finite; a program needn't handle non-finite values.
Results may differ from a plain program's by a relative error of at most 0.0058.
Values may be sent and summed in bfloat16 or wider, within the bound.
No kernel may reach another device: no remote copies, remote signals or barrier semaphores. Data moves between devices by JAX's collectives and lax.ppermute only.
A program may use at most 128 MiB of HBM per device.

v0:
```python
import functools

import jax
import jax.numpy as jnp
from jax import lax
from jax.experimental import pallas as pl
from jax.experimental.pallas import tpu as pltpu
from jax.sharding import PartitionSpec as P

AXES = ("node", "local")
CHUNKS = ((0, 4), (4, 2))
VMEM_LIMIT = 60 * 1024 * 1024


def params():
    return pltpu.CompilerParams(dimension_semantics=("arbitrary",), vmem_limit_bytes=VMEM_LIMIT)


def pack_body(slot_ref, x_ref, y_ref, out_ref, pick_ref, *, first, count, half):
    step = pl.program_id(0)
    experts, tok_rows = slot_ref.shape

    @pl.when(step == 0)
    def _():
        shape = (experts, count, tok_rows)
        wanted = first + lax.broadcasted_iota(jnp.int32, shape, 1)
        slots = jnp.broadcast_to(slot_ref[...][:, None, :], shape)
        picked = jnp.where(slots == wanted, 1.0, 0.0)
        pick_ref[...] = picked.reshape(experts * count, tok_rows).astype(jnp.bfloat16)

    def emit(rows):
        block = jnp.dot(pick_ref[...], rows, preferred_element_type=jnp.float32)
        out_ref[...] = block.astype(jnp.bfloat16).reshape(out_ref.shape)

    @pl.when(step < half)
    def _():
        emit(x_ref[...])

    @pl.when(step >= half)
    def _():
        emit(y_ref[...])


def pack(slot_by_expert, x, y, first, count, block=896):
    experts, tok_rows = slot_by_expert.shape
    width = x.shape[1]
    half = width // block
    return pl.pallas_call(
        functools.partial(pack_body, first=first, count=count, half=half),
        grid=(2 * half,),
        in_specs=[
            pl.BlockSpec((experts, tok_rows), lambda j: (0, 0)),
            pl.BlockSpec((tok_rows, block), lambda j: (0, jnp.minimum(j, half - 1))),
            pl.BlockSpec((tok_rows, block), lambda j: (0, jnp.maximum(j - half, 0))),
        ],
        out_specs=pl.BlockSpec((experts, count, block), lambda j: (0, 0, j)),
        out_shape=jax.ShapeDtypeStruct((experts, count, 2 * width), jnp.bfloat16),
        scratch_shapes=[pltpu.VMEM((experts * count, tok_rows), jnp.bfloat16)],
        compiler_params=params(),
        name="pack",
    )(slot_by_expert, x, y)


def expert_body(
    x_ref, y_ref, gate_ref, up_ref, down_ref, out_ref,
    gate_acc, up_acc, back_acc, d_gate_ref, d_up_ref, *, steps,
):
    step = pl.program_id(0)
    rows = gate_acc.shape[0]
    block = x_ref.shape[2]
    across = (((1,), (1,)), ((), ()))

    def add(acc, value, start):
        if start:
            acc[...] = value
        else:
            acc[...] += value

    def forward(start):
        x = x_ref[...].reshape(rows, block)
        y = y_ref[...].reshape(rows, block)
        add(gate_acc, jnp.dot(x, gate_ref[...], preferred_element_type=jnp.float32), start)
        add(up_acc, jnp.dot(x, up_ref[...], preferred_element_type=jnp.float32), start)
        add(back_acc, lax.dot_general(y, down_ref[...], across, preferred_element_type=jnp.float32), start)

    @pl.when(step == 0)
    def _():
        forward(True)

    @pl.when((step > 0) & (step < steps))
    def _():
        forward(False)

    @pl.when(step == steps - 1)
    def _():
        gate_pre = gate_acc[...]
        up_pre = up_acc[...]
        back = back_acc[...]
        sig = 1.0 / (1.0 + jnp.exp(-gate_pre))
        d_gate_ref[...] = (back * up_pre * sig * (1.0 + gate_pre * (1.0 - sig))).astype(jnp.bfloat16)
        d_up_ref[...] = (back * gate_pre * sig).astype(jnp.bfloat16)

    @pl.when(step >= steps)
    def _():
        total = lax.dot_general(d_gate_ref[...], gate_ref[...], across, preferred_element_type=jnp.float32)
        total += lax.dot_general(d_up_ref[...], up_ref[...], across, preferred_element_type=jnp.float32)
        out_ref[...] = total.astype(jnp.bfloat16).reshape(out_ref.shape)


def expert(arrived, w_gate, w_up, w_down, block=512):
    sources, count, double = arrived.shape
    width = double // 2
    hidden = w_gate.shape[1]
    rows = sources * count
    steps = width // block
    there = lambda j: jnp.minimum(j, steps - 1)
    back = lambda j: jnp.where(j < steps, j, 2 * steps - 1 - j)
    return pl.pallas_call(
        functools.partial(expert_body, steps=steps),
        grid=(2 * steps,),
        in_specs=[
            pl.BlockSpec((sources, count, block), lambda j: (0, 0, there(j))),
            pl.BlockSpec((sources, count, block), lambda j: (0, 0, steps + there(j))),
            pl.BlockSpec((block, hidden), lambda j: (back(j), 0)),
            pl.BlockSpec((block, hidden), lambda j: (back(j), 0)),
            pl.BlockSpec((hidden, block), lambda j: (0, there(j))),
        ],
        out_specs=pl.BlockSpec(
            (sources, count, block), lambda j: (0, 0, jnp.where(j < steps, steps - 1, 2 * steps - 1 - j))
        ),
        out_shape=jax.ShapeDtypeStruct((sources, count, width), jnp.bfloat16),
        scratch_shapes=[pltpu.VMEM((rows, hidden), jnp.float32)] * 3
        + [pltpu.VMEM((rows, hidden), jnp.bfloat16)] * 2,
        compiler_params=params(),
        cost_estimate=pl.CostEstimate(
            flops=10 * rows * width * hidden,
            transcendentals=rows * hidden,
            bytes_accessed=2 * (5 * width * hidden + 3 * rows * width),
        ),
        name="expert",
    )(arrived, arrived, w_gate, w_up, w_down)


def combine_body(slot_ref, weight_ref, block_ref, *refs, first, count, last):
    prior_ref, out_ref, scale_ref = (refs if last else (None,) + refs)
    tok_rows, experts = slot_ref.shape
    wide = experts * count

    @pl.when(pl.program_id(0) == 0)
    def _():
        for j in range(count):
            scale = jnp.where(slot_ref[...] == first + j, weight_ref[...], 0.0)
            high = scale.astype(jnp.bfloat16)
            low = (scale - high.astype(jnp.float32)).astype(jnp.bfloat16)
            scale_ref[j, 0:tok_rows, :] = high
            scale_ref[j, tok_rows : 2 * tok_rows, :] = low

    total = jnp.zeros((2 * tok_rows, block_ref.shape[2]), jnp.float32)
    for j in range(count):
        total += jnp.dot(scale_ref[j], block_ref[:, j, :], preferred_element_type=jnp.float32)
    total = total[0:tok_rows] + total[tok_rows : 2 * tok_rows]
    if last:
        total = total + prior_ref[...]
    out_ref[...] = total.astype(out_ref.dtype)


def combine(slot, weight, returned, prior, first, count, block=896):
    tok_rows, experts = slot.shape
    width = returned.shape[2]
    last = prior is not None
    whole = pl.BlockSpec((tok_rows, experts), lambda j: (0, 0))
    part = pl.BlockSpec((tok_rows, block), lambda j: (0, j))
    operands = (slot, weight, returned) + ((prior,) if last else ())
    return pl.pallas_call(
        functools.partial(combine_body, first=first, count=count, last=last),
        grid=(width // block,),
        in_specs=[whole, whole, pl.BlockSpec((experts, count, block), lambda j: (0, 0, j))]
        + ([part] if last else []),
        out_specs=part,
        out_shape=jax.ShapeDtypeStruct((tok_rows, width), jnp.bfloat16 if last else jnp.float32),
        scratch_shapes=[pltpu.VMEM((count, 2 * tok_rows, experts), jnp.bfloat16)],
        compiler_params=params(),
        name="combine",
    )(*operands)


def exchange(block):
    return lax.all_to_all(block, AXES, split_axis=0, concat_axis=0, tiled=True)


def body(tokens_in, grad_out, expert_ids, gate_weights, w_gate, w_up, w_down):
    tok_rows = tokens_in.shape[0]
    experts = lax.axis_size("node") * lax.axis_size("local")
    numbers = jnp.arange(experts, dtype=jnp.int32)
    named = expert_ids[:, :, None] == numbers[None, None, :]
    member = jnp.any(named, axis=1)
    weight = jnp.sum(jnp.where(named, gate_weights[:, :, None], 0.0), axis=1)
    order = jnp.arange(tok_rows, dtype=jnp.int32)
    earlier = (order[:, None] > order[None, :]).astype(jnp.bfloat16)
    slot = jnp.dot(earlier, member.astype(jnp.bfloat16), preferred_element_type=jnp.float32)
    slot = jnp.where(member, slot, -1.0).astype(jnp.int32)
    slot_by_expert = slot.T
    (first_a, count_a), (first_b, count_b) = CHUNKS
    payload_a = pack(slot_by_expert, tokens_in, grad_out, first_a, count_a)
    payload_a, slot_late = lax.optimization_barrier((payload_a, slot_by_expert))
    arrived_a = exchange(payload_a)
    payload_b = pack(slot_late, tokens_in, grad_out, first_b, count_b)
    arrived_b = exchange(payload_b)
    result_a = expert(arrived_a, w_gate[0], w_up[0], w_down[0])
    returned_a = exchange(result_a)
    result_b = expert(arrived_b, w_gate[0], w_up[0], w_down[0])
    returned_b = exchange(result_b)
    total = combine(slot, weight, returned_a, None, first_a, count_a)
    return combine(slot, weight, returned_b, total, first_b, count_b)


def solution(mesh):
    rows = P(AXES, None)
    cube = P(AXES, None, None)
    in_specs = (rows, rows, rows, rows, cube, cube, cube)
    return jax.shard_map(body, mesh=mesh, in_specs=in_specs, out_specs=rows, check_vma=False)
```

profile of v0, /device:TPU:1, one launch (start us, length us, event | category | flops | bytes accessed | tf_op | source)
XLA Modules:
  0.0 261.7 jit_solution(15490349562189142658)
XLA Ops:
  0.0 0.8 fusion.1
  0.8 0.1 fusion.slot_ref
  1.0 0.0 copy-start.1
  1.0 0.7 copy.12.slot_ref
  1.7 8.2 %pack.2 = bf16[128,4,7168]{2,1,0:T(4,128)(2,1)} custom-call(s32[128,128]{1,0:T(8,128)} %copy.12.slot_ref, bf16[128,3584]{1,0:T(8,128)(2,1)} %x_ref.3, bf16[128,3584]{1,0:T(8,128)(2,1)} %y_ref.3), custom_call_target="tpu_custom_call" | custom-call | tf_op jit(solution)/shard_map/pack/pallas_call | solution.py:48
  9.9 11.9 %all-to-all-start.2 = ((bf16[128,4,7168]{2,1,0:T(4,128)(2,1)}), bf16[128,4,7168]{2,1,0:T(4,128)(2,1)}, u32[]{:S(2)}, u32[]{:S(2)}) async-start(bf16[128,4,7168]{2,1,0:T(4,128)(2,1)} %pack.2), calls=%async_computation.2 | async-start | bytes 14680064 | tf_op jit(solution)/shard_map/all_to_all | solution.py:188
  21.8 0.0 copy-done.1
  21.9 0.7 copy.13.slot_ref
  22.6 7.3 %pack.3 = bf16[128,2,7168]{2,1,0:T(2,128)(2,1)} custom-call(s32[128,128]{1,0:T(8,128)} %copy.13.slot_ref, bf16[128,3584]{1,0:T(8,128)(2,1)} %x_ref.3, bf16[128,3584]{1,0:T(8,128)(2,1)} %y_ref.3), custom_call_target="tpu_custom_call" | custom-call | tf_op jit(solution)/shard_map/pack/pallas_call | solution.py:48
  29.9 81.0 %all-to-all-done.2.x_ref.y_ref = bf16[128,4,7168]{2,1,0:T(4,128)(2,1)} async-done(((bf16[128,4,7168]{2,1,0:T(4,128)(2,1)}), bf16[128,4,7168]{2,1,0:T(4,128)(2,1)}, u32[]{:S(2)}, u32[]{:S(2)}) %all-to-all-start.2) | async-done | bytes 7340064 | tf_op jit(solution)/shard_map/all_to_all | solution.py:188
  110.9 11.4 %all-to-all-start = ((bf16[128,2,7168]{2,1,0:T(2,128)(2,1)}), bf16[128,2,7168]{2,1,0:T(2,128)(2,1)}, u32[]{:S(2)}, u32[]{:S(2)}) async-start(bf16[128,2,7168]{2,1,0:T(2,128)(2,1)} %pack.3), calls=%async_computation | async-start | bytes 7340032 | tf_op jit(solution)/shard_map/all_to_all | solution.py:188
  122.3 28.7 %expert.3 = bf16[128,4,3584]{2,1,0:T(4,128)(2,1)} custom-call(bf16[128,4,7168]{2,1,0:T(4,128)(2,1)} %all-to-all-done.2.x_ref.y_ref, bf16[128,4,7168]{2,1,0:T(4,128)(2,1)} %all-to-all-done.2.x_ref.y_ref, bf16[3584,1024]{1,0:T(8,128)(2,1)} %bitcast.7, bf16[3584,1024]{1,0:T(8,128)(2,1)} %bitcast.9, bf16[1024,3584]{1,0:T(8,128)(2,1)} %bitcast.11), custom_call_target="tpu_custom_call" | custom-call | flops 18790481920 | bytes 47710208 | tf_op jit(solution)/shard_map/expert/pallas_call | solution.py:118
  151.0 18.6 %all-to-all-done.x_ref.y_ref = bf16[128,2,7168]{2,1,0:T(2,128)(2,1)} async-done(((bf16[128,2,7168]{2,1,0:T(2,128)(2,1)}), bf16[128,2,7168]{2,1,0:T(2,128)(2,1)}, u32[]{:S(2)}, u32[]{:S(2)}) %all-to-all-start) | async-done | bytes 3670048 | tf_op jit(solution)/shard_map/all_to_all | solution.py:188
  169.6 4.8 %all-to-all-start.3 = ((bf16[128,4,3584]{2,1,0:T(4,128)(2,1)}), bf16[128,4,3584]{2,1,0:T(4,128)(2,1)}, u32[]{:S(2)}, u32[]{:S(2)}) async-start(bf16[128,4,3584]{2,1,0:T(4,128)(2,1)} %expert.3), calls=%async_computation.3 | async-start | bytes 7340032 | tf_op jit(solution)/shard_map/all_to_all | solution.py:188
  174.4 22.2 %expert.2 = bf16[128,2,3584]{2,1,0:T(2,128)(2,1)} custom-call(bf16[128,2,7168]{2,1,0:T(2,128)(2,1)} %all-to-all-done.x_ref.y_ref, bf16[128,2,7168]{2,1,0:T(2,128)(2,1)} %all-to-all-done.x_ref.y_ref, bf16[3584,1024]{1,0:T(8,128)(2,1)} %bitcast.8, bf16[3584,1024]{1,0:T(8,128)(2,1)} %bitcast.10, bf16[1024,3584]{1,0:T(8,128)(2,1)} %bitcast.12), custom_call_target="tpu_custom_call" | custom-call | flops 9395240960 | bytes 42205184 | tf_op jit(solution)/shard_map/expert/pallas_call | solution.py:118
  196.6 0.0 copy-start.2
  196.6 0.0 copy-start.3
  196.6 25.3 %all-to-all-done.3.block_ref = bf16[128,4,3584]{2,1,0:T(4,128)(2,1)} async-done(((bf16[128,4,3584]{2,1,0:T(4,128)(2,1)}), bf16[128,4,3584]{2,1,0:T(4,128)(2,1)}, u32[]{:S(2)}, u32[]{:S(2)}) %all-to-all-start.3) | async-done | bytes 3670048 | tf_op jit(solution)/shard_map/all_to_all | solution.py:188
  221.9 3.8 %all-to-all-start.1 = ((bf16[128,2,3584]{2,1,0:T(2,128)(2,1)}), bf16[128,2,3584]{2,1,0:T(2,128)(2,1)S(1)}, u32[]{:S(2)}, u32[]{:S(2)}) async-start(bf16[128,2,3584]{2,1,0:T(2,128)(2,1)} %expert.2), calls=%async_computation.1 | async-start | bytes 3670016 | tf_op jit(solution)/shard_map/all_to_all | solution.py:188
  225.7 0.0 copy-done.2
  225.7 0.0 copy-done.3
  225.7 0.8 select_reduce_fusion.weight_ref
  226.5 9.8 %combine.2.refs_0_ = f32[128,3584]{1,0:T(8,128)} custom-call(s32[128,128]{1,0:T(8,128)} %copy-done.1, f32[128,128]{1,0:T(8,128)} %select_reduce_fusion.weight_ref, bf16[128,4,3584]{2,1,0:T(4,128)(2,1)} %all-to-all-done.3.block_ref), custom_call_target="tpu_custom_call" | custom-call | tf_op jit(solution)/shard_map/combine/pallas_call | solution.py:174
  236.4 17.4 %all-to-all-done.1.block_ref = bf16[128,2,3584]{2,1,0:T(2,128)(2,1)S(1)} async-done(((bf16[128,2,3584]{2,1,0:T(2,128)(2,1)}), bf16[128,2,3584]{2,1,0:T(2,128)(2,1)S(1)}, u32[]{:S(2)}, u32[]{:S(2)}) %all-to-all-start.1) | async-done | bytes 1835040 | tf_op jit(solution)/shard_map/all_to_all | solution.py:188
  253.8 0.0 copy-start
  253.8 1.2 copy-done
  255.0 6.7 %combine.3 = bf16[128,3584]{1,0:T(8,128)(2,1)} custom-call(s32[128,128]{1,0:T(8,128)} %copy-done.1, f32[128,128]{1,0:T(8,128)} %select_reduce_fusion.weight_ref, bf16[128,2,3584]{2,1,0:T(2,128)(2,1)} %copy-done, f32[128,3584]{1,0:T(8,128)} %combine.2.refs_0_), custom_call_target="tpu_custom_call" | custom-call | tf_op jit(solution)/shard_map/combine/pallas_call | solution.py:174
Async XLA Ops:
  1.0 20.9 %copy-start.1 = (s32[128,128]{1,0:T(8,128)}, s32[128,128]{1,0:T(8,128)S(1)}, u32[]{:S(2)}) copy-start(s32[128,128]{1,0:T(8,128)S(1)} %fusion.slot_ref) | copy-start | bytes 196612
  9.9 100.9 %all-to-all-start.2 = ((bf16[128,4,7168]{2,1,0:T(4,128)(2,1)}), bf16[128,4,7168]{2,1,0:T(4,128)(2,1)}, u32[]{:S(2)}, u32[]{:S(2)}) async-start(bf16[128,4,7168]{2,1,0:T(4,128)(2,1)} %pack.2), calls=%async_computation.2 | async-start | bytes 14680064 | tf_op jit(solution)/shard_map/all_to_all | solution.py:188
  110.9 58.7 %all-to-all-start = ((bf16[128,2,7168]{2,1,0:T(2,128)(2,1)}), bf16[128,2,7168]{2,1,0:T(2,128)(2,1)}, u32[]{:S(2)}, u32[]{:S(2)}) async-start(bf16[128,2,7168]{2,1,0:T(2,128)(2,1)} %pack.3), calls=%async_computation | async-start | bytes 7340032 | tf_op jit(solution)/shard_map/all_to_all | solution.py:188
  169.6 52.3 %all-to-all-start.3 = ((bf16[128,4,3584]{2,1,0:T(4,128)(2,1)}), bf16[128,4,3584]{2,1,0:T(4,128)(2,1)}, u32[]{:S(2)}, u32[]{:S(2)}) async-start(bf16[128,4,3584]{2,1,0:T(4,128)(2,1)} %expert.3), calls=%async_computation.3 | async-start | bytes 7340032 | tf_op jit(solution)/shard_map/all_to_all | solution.py:188
  196.6 29.1 %copy-start.2 = (s32[128,3]{0,1:T(4,128)S(1)}, s32[128,3]{0,1:T(4,128)}, u32[]{:S(2)}) copy-start(s32[128,3]{0,1:T(4,128)} %param.9) | copy-start | bytes 4612
  196.6 29.1 %copy-start.3 = (f32[128,3]{0,1:T(4,128)S(1)}, f32[128,3]{0,1:T(4,128)}, u32[]{:S(2)}) copy-start(f32[128,3]{0,1:T(4,128)} %param.10) | copy-start | bytes 4612
  221.9 31.9 %all-to-all-start.1 = ((bf16[128,2,3584]{2,1,0:T(2,128)(2,1)}), bf16[128,2,3584]{2,1,0:T(2,128)(2,1)S(1)}, u32[]{:S(2)}, u32[]{:S(2)}) async-start(bf16[128,2,3584]{2,1,0:T(2,128)(2,1)} %expert.2), calls=%async_computation.1 | async-start | bytes 3670016 | tf_op jit(solution)/shard_map/all_to_all | solution.py:188
  253.8 1.2 copy-start
where the time goes:
time: 263 us; the launch traced here: 262 us
  waiting for transfers between devices  142 us (54%)
  Pallas kernels  83 us (32%)
  starting transfers between devices  31.9 us (12%)
  local copies, waits for them, and re-layouts  2.72 us (1%)
    all_to_all x4, waiting for transfers between devices, exchange(): return lax.all_to_all(block, AXES, split_axis=0, concat_axis=0, tiled=True)  142 us
    pallas_call x2, Pallas kernels, expert(): pl.pallas_call(functools.partial(expert_body, steps=steps), grid=(2 * ste...  50.9 us
    all_to_all x4, starting transfers between devices, exchange(): return lax.all_to_all(block, AXES, split_axis=0, concat_axis=0, tiled=True)  31.9 us
    pallas_call x2, Pallas kernels, combine(): pl.pallas_call(functools.partial(combine_body, first=first, count=count,...  16.5 us
    pallas_call x2, Pallas kernels, pack(): pl.pallas_call(functools.partial(pack_body, first=first, count=count, hal...  15.6 us
  transfers between devices with their start and end apart: 4, of which 4 were waited for; matrix products, arithmetic and copies ran while one was open for 1% of the time, Pallas kernels for 26%

commit v1 on v0

v1 whole, which is shorter than its diff:
```python
import functools

import jax
import jax.numpy as jnp
from jax import lax
from jax.experimental import pallas as pl
from jax.experimental.pallas import tpu as pltpu
from jax.sharding import PartitionSpec as P

AXES = ("node", "local")
CHUNKS = ((0, 4), (4, 2))
VMEM_LIMIT = 60 * 1024 * 1024
ACROSS = (((1,), (1,)), ((), ()))


def params():
    return pltpu.CompilerParams(dimension_semantics=("arbitrary",), vmem_limit_bytes=VMEM_LIMIT)


def slots_of(ids_ref, experts):
    topk, tok_rows = ids_ref.shape
    numbers = lax.broadcasted_iota(jnp.int32, (experts, tok_rows), 0)
    member = ids_ref[0:1, :] == numbers
    for k in range(1, topk):
        member = member | (ids_ref[k : k + 1, :] == numbers)
    source = lax.broadcasted_iota(jnp.int32, (tok_rows, tok_rows), 0)
    target = lax.broadcasted_iota(jnp.int32, (tok_rows, tok_rows), 1)
    before = jnp.where(source < target, 1.0, 0.0).astype(jnp.bfloat16)
    flags = jnp.where(member, 1.0, 0.0).astype(jnp.bfloat16)
    slot = jnp.dot(flags, before, preferred_element_type=jnp.float32)
    return jnp.where(member, slot, -1.0)


def pack_body(ids_ref, x_ref, y_ref, out_ref, pick_ref, *, first, count, experts):
    tok_rows = ids_ref.shape[1]

    @pl.when(pl.program_id(0) == 0)
    def _():
        shape = (experts, 2 * count, 2 * tok_rows)
        slot = slots_of(ids_ref, experts)
        slot = jnp.concatenate([slot, slot], axis=1)
        row = lax.broadcasted_iota(jnp.int32, shape, 1)
        column = lax.broadcasted_iota(jnp.int32, shape, 2)
        wanted = (first + row % count).astype(jnp.float32)
        same = (row >= count) == (column >= tok_rows)
        hit = same & (jnp.broadcast_to(slot[:, None, :], shape) == wanted)
        picked = jnp.where(hit, 1.0, 0.0)
        pick_ref[...] = picked.reshape(experts * 2 * count, 2 * tok_rows).astype(jnp.bfloat16)

    both = jnp.concatenate([x_ref[...], y_ref[...]], axis=0)
    block = jnp.dot(pick_ref[...], both, preferred_element_type=jnp.float32)
    out_ref[...] = block.astype(jnp.bfloat16).reshape(out_ref.shape)


def pack(ids, x, y, experts, first, count, block=1792):
    topk, tok_rows = ids.shape
    width = x.shape[1]
    part = pl.BlockSpec((tok_rows, block), lambda j: (0, j))
    return pl.pallas_call(
        functools.partial(pack_body, first=first, count=count, experts=experts),
        grid=(width // block,),
        in_specs=[pl.BlockSpec((topk, tok_rows), lambda j: (0, 0)), part, part],
        out_specs=pl.BlockSpec((experts, 2 * count, block), lambda j: (0, 0, j)),
        out_shape=jax.ShapeDtypeStruct((experts, 2 * count, width), jnp.bfloat16),
        scratch_shapes=[pltpu.VMEM((experts * 2 * count, 2 * tok_rows), jnp.bfloat16)],
        compiler_params=params(),
        name="pack",
    )(ids, x, y)


def expert_body(
    in_ref, gate_ref, up_ref, down_ref, out_ref,
    gate_acc, up_acc, back_acc, d_gate_ref, d_up_ref, *, steps,
):
    step = pl.program_id(0)
    rows = gate_acc.shape[0]
    count = in_ref.shape[1] // 2
    block = in_ref.shape[2]

    def add(acc, value, start):
        if start:
            acc[...] = value
        else:
            acc[...] += value

    def forward(start):
        x = in_ref[:, 0:count, :].reshape(rows, block)
        y = in_ref[:, count : 2 * count, :].reshape(rows, block)
        add(gate_acc, jnp.dot(x, gate_ref[...], preferred_element_type=jnp.float32), start)
        add(up_acc, jnp.dot(x, up_ref[...], preferred_element_type=jnp.float32), start)
        add(back_acc, lax.dot_general(y, down_ref[...], ACROSS, preferred_element_type=jnp.float32), start)

    @pl.when(step == 0)
    def _():
        forward(True)

    @pl.when((step > 0) & (step < steps))
    def _():
        forward(False)

    @pl.when(step == steps - 1)
    def _():
        gate_pre = gate_acc[...]
        up_pre = up_acc[...]
        back = back_acc[...]
        sig = 1.0 / (1.0 + jnp.exp(-gate_pre))
        d_gate_ref[...] = (back * up_pre * sig * (1.0 + gate_pre * (1.0 - sig))).astype(jnp.bfloat16)
        d_up_ref[...] = (back * gate_pre * sig).astype(jnp.bfloat16)

    @pl.when(step >= steps)
    def _():
        total = lax.dot_general(d_gate_ref[...], gate_ref[...], ACROSS, preferred_element_type=jnp.float32)
        total += lax.dot_general(d_up_ref[...], up_ref[...], ACROSS, preferred_element_type=jnp.float32)
        out_ref[...] = total.astype(jnp.bfloat16).reshape(out_ref.shape)


def expert(arrived, w_gate, w_up, w_down, block=512):
    sources, double, width = arrived.shape
    count = double // 2
    hidden = w_gate.shape[1]
    rows = sources * count
    steps = width // block
    there = lambda j: jnp.minimum(j, steps - 1)
    back = lambda j: jnp.where(j < steps, j, 2 * steps - 1 - j)
    return pl.pallas_call(
        functools.partial(expert_body, steps=steps),
        grid=(2 * steps,),
        in_specs=[
            pl.BlockSpec((sources, double, block), lambda j: (0, 0, there(j))),
            pl.BlockSpec((block, hidden), lambda j: (back(j), 0)),
            pl.BlockSpec((block, hidden), lambda j: (back(j), 0)),
            pl.BlockSpec((hidden, block), lambda j: (0, there(j))),
        ],
        out_specs=pl.BlockSpec(
            (sources, count, block), lambda j: (0, 0, jnp.where(j < steps, steps - 1, 2 * steps - 1 - j))
        ),
        out_shape=jax.ShapeDtypeStruct((sources, count, width), jnp.bfloat16),
        scratch_shapes=[pltpu.VMEM((rows, hidden), jnp.float32)] * 3
        + [pltpu.VMEM((rows, hidden), jnp.bfloat16)] * 2,
        compiler_params=params(),
        cost_estimate=pl.CostEstimate(
            flops=10 * rows * width * hidden,
            transcendentals=rows * hidden,
            bytes_accessed=2 * (5 * width * hidden + 3 * rows * width),
        ),
        name="expert",
    )(arrived, w_gate, w_up, w_down)


def scale_of(slot, weight, first, count):
    experts, tok_rows = slot.shape
    shape = (experts, count, tok_rows)
    wanted = (first + lax.broadcasted_iota(jnp.int32, shape, 1)).astype(jnp.float32)
    hit = jnp.broadcast_to(slot[:, None, :], shape) == wanted
    scale = jnp.where(hit, jnp.broadcast_to(weight[:, None, :], shape), 0.0)
    scale = scale.reshape(experts * count, tok_rows).T
    high = scale.astype(jnp.bfloat16)
    low = (scale - high.astype(jnp.float32)).astype(jnp.bfloat16)
    return jnp.concatenate([high, low], axis=0)


def weighted(scale_ref, block_ref):
    flat = block_ref[...].reshape(scale_ref.shape[1], block_ref.shape[2])
    total = jnp.dot(scale_ref[...], flat, preferred_element_type=jnp.float32)
    tok_rows = total.shape[0] // 2
    return total[0:tok_rows] + total[tok_rows:]


def combine_a_body(ids_ref, gates_ref, block_ref, total_ref, late_ref, scale_ref, *, chunks, experts):
    topk, tok_rows = ids_ref.shape

    @pl.when(pl.program_id(0) == 0)
    def _():
        slot = slots_of(ids_ref, experts)
        numbers = lax.broadcasted_iota(jnp.int32, (experts, tok_rows), 0)
        weight = jnp.zeros((experts, tok_rows), jnp.float32)
        for k in range(topk):
            weight = jnp.where(ids_ref[k : k + 1, :] == numbers, gates_ref[k : k + 1, :], weight)
        scale_ref[...] = scale_of(slot, weight, *chunks[0])
        late_ref[...] = scale_of(slot, weight, *chunks[1])

    total_ref[...] = weighted(scale_ref, block_ref)


def combine_a(ids, gates, returned, chunks, block=896):
    topk, tok_rows = ids.shape
    experts, count, width = returned.shape
    whole = pl.BlockSpec((topk, tok_rows), lambda j: (0, 0))
    late = (2 * tok_rows, experts * chunks[1][1])
    return pl.pallas_call(
        functools.partial(combine_a_body, chunks=chunks, experts=experts),
        grid=(width // block,),
        in_specs=[whole, whole, pl.BlockSpec((experts, count, block), lambda j: (0, 0, j))],
        out_specs=[
            pl.BlockSpec((tok_rows, block), lambda j: (0, j)),
            pl.BlockSpec(late, lambda j: (0, 0)),
        ],
        out_shape=[
            jax.ShapeDtypeStruct((tok_rows, width), jnp.float32),
            jax.ShapeDtypeStruct(late, jnp.bfloat16),
        ],
        scratch_shapes=[pltpu.VMEM((2 * tok_rows, experts * count), jnp.bfloat16)],
        compiler_params=params(),
        name="combine_first",
    )(ids, gates, returned)


def combine_b_body(scale_ref, block_ref, prior_ref, out_ref):
    block = out_ref.shape[1]
    start = pl.multiple_of(pl.program_id(0) * block, 128)
    part = block_ref.at[:, :, pl.ds(start, block)]
    out_ref[...] = (prior_ref[...] + weighted(scale_ref, part)).astype(jnp.bfloat16)


def combine_b(scale, returned, prior, block=1792):
    experts, count, width = returned.shape
    tok_rows = prior.shape[0]
    part = pl.BlockSpec((tok_rows, block), lambda j: (0, j))
    return pl.pallas_call(
        combine_b_body,
        grid=(width // block,),
        in_specs=[
            pl.BlockSpec(scale.shape, lambda j: (0, 0)),
            pl.BlockSpec(memory_space=pltpu.VMEM),
            part,
        ],
        out_specs=part,
        out_shape=jax.ShapeDtypeStruct((tok_rows, width), jnp.bfloat16),
        compiler_params=params(),
        name="combine_last",
    )(scale, returned, prior)


def exchange(block):
    return lax.all_to_all(block, AXES, split_axis=0, concat_axis=0, tiled=True)


def body(tokens_in, grad_out, expert_ids, gate_weights, w_gate, w_up, w_down):
    experts = lax.axis_size("node") * lax.axis_size("local")
    ids = expert_ids.T
    gates = gate_weights.T
    (first_a, count_a), (first_b, count_b) = CHUNKS
    payload_a = pack(ids, tokens_in, grad_out, experts, first_a, count_a)
    payload_a, ids_late = lax.optimization_barrier((payload_a, ids))
    arrived_a = exchange(payload_a)
    payload_b = pack(ids_late, tokens_in, grad_out, experts, first_b, count_b)
    arrived_b = exchange(payload_b)
    result_a = expert(arrived_a, w_gate[0], w_up[0], w_down[0])
    returned_a = exchange(result_a)
    result_b = expert(arrived_b, w_gate[0], w_up[0], w_down[0])
    returned_b = exchange(result_b)
    total, scale_b = combine_a(ids, gates, returned_a, CHUNKS)
    returned_b = pltpu.with_memory_space_constraint(returned_b, pltpu.VMEM)
    return combine_b(scale_b, returned_b, total)


def solution(mesh):
    rows = P(AXES, None)
    cube = P(AXES, None, None)
    in_specs = (rows, rows, rows, rows, cube, cube, cube)
    return jax.shard_map(body, mesh=mesh, in_specs=in_specs, out_specs=rows, check_vma=False)
```

time: 263 us -> 253 us (0.962)
  Pallas kernels: 83 us -> 68.8 us
  waiting for transfers between devices: 142 us -> 152 us
  local copies, waits for them, and re-layouts: 2.72 us -> 0 us
    pallas_call x4, Pallas kernels: 32.1 us -> 17.9 us  [the longest x2 9.73 us: pack(): pl.pallas_call(functools.partial(pack_body, first=first, count=count, exp...]
    all_to_all x4, waiting for transfers between devices: 142 us -> 152 us  [exchange(): return lax.all_to_all(block, AXES, split_axis=0, concat_axis=0, tiled=True)]
  transfers between devices with their start and end apart: 4 -> 4, of which waited for: 4 -> 4; matrix products, arithmetic and copies ran while one was open for 1% -> 0% of each run, Pallas kernels for 26% -> 24%
where the time goes in v1:
time: 253 us; the launch traced here: 252 us
  waiting for transfers between devices  152 us (60%)
  Pallas kernels  68.8 us (27%)
  starting transfers between devices  31.9 us (13%)
    all_to_all x4, waiting for transfers between devices, exchange(): return lax.all_to_all(block, AXES, split_axis=0, concat_axis=0, tiled=True)  152 us
    pallas_call x2, Pallas kernels, expert(): pl.pallas_call(functools.partial(expert_body, steps=steps), grid=(2 * ste...  50.8 us
    all_to_all x4, starting transfers between devices, exchange(): return lax.all_to_all(block, AXES, split_axis=0, concat_axis=0, tiled=True)  31.9 us
    pallas_call x2, Pallas kernels, pack(): pl.pallas_call(functools.partial(pack_body, first=first, count=count, exp...  9.73 us
    pallas_call x1, Pallas kernels, combine_a(): pl.pallas_call(functools.partial(combine_a_body, chunks=chunks, experts=e...  5.34 us
  transfers between devices with their start and end apart: 4, of which 4 were waited for; matrix products, arithmetic and copies ran while one was open for 0% of the time, Pallas kernels for 24%

profile of v1, /device:TPU:1, one launch (start us, length us, event | category | flops | bytes accessed | tf_op | source)
XLA Modules:
  0.0 252.3 jit_solution(12457622214314235684)
XLA Ops:
  0.0 5.6 %pack.2 = bf16[128,8,3584]{2,1,0:T(8,128)(2,1)} custom-call(s32[3,128]{1,0:T(4,128)} %bitcast.5, bf16[128,3584]{1,0:T(8,128)(2,1)} %x_ref.3, bf16[128,3584]{1,0:T(8,128)(2,1)} %y_ref.3), custom_call_target="tpu_custom_call" | custom-call | tf_op jit(solution)/shard_map/pack/pallas_call | solution.py:59
  5.6 11.9 %all-to-all-start = ((bf16[128,8,3584]{2,1,0:T(8,128)(2,1)}), bf16[128,8,3584]{2,1,0:T(8,128)(2,1)}, u32[]{:S(2)}, u32[]{:S(2)}) async-start(bf16[128,8,3584]{2,1,0:T(8,128)(2,1)} %pack.2), calls=%async_computation | async-start | bytes 14680064 | tf_op jit(solution)/shard_map/all_to_all | solution.py:235
  17.5 4.1 %pack.3 = bf16[128,4,3584]{2,1,0:T(4,128)(2,1)} custom-call(s32[3,128]{1,0:T(4,128)} %bitcast.6, bf16[128,3584]{1,0:T(8,128)(2,1)} %x_ref.3, bf16[128,3584]{1,0:T(8,128)(2,1)} %y_ref.3), custom_call_target="tpu_custom_call" | custom-call | tf_op jit(solution)/shard_map/pack/pallas_call | solution.py:59
  21.6 84.9 %all-to-all-done.in_ref = bf16[128,8,3584]{2,1,0:T(8,128)(2,1)} async-done(((bf16[128,8,3584]{2,1,0:T(8,128)(2,1)}), bf16[128,8,3584]{2,1,0:T(8,128)(2,1)}, u32[]{:S(2)}, u32[]{:S(2)}) %all-to-all-start) | async-done | bytes 7340064 | tf_op jit(solution)/shard_map/all_to_all | solution.py:235
  106.5 11.4 %all-to-all-start.2 = ((bf16[128,4,3584]{2,1,0:T(4,128)(2,1)}), bf16[128,4,3584]{2,1,0:T(4,128)(2,1)}, u32[]{:S(2)}, u32[]{:S(2)}) async-start(bf16[128,4,3584]{2,1,0:T(4,128)(2,1)} %pack.3), calls=%async_computation.2 | async-start | bytes 7340032 | tf_op jit(solution)/shard_map/all_to_all | solution.py:235
  117.9 28.7 %expert.2 = bf16[128,4,3584]{2,1,0:T(4,128)(2,1)} custom-call(bf16[128,8,3584]{2,1,0:T(8,128)(2,1)} %all-to-all-done.in_ref, bf16[3584,1024]{1,0:T(8,128)(2,1)} %bitcast.9, bf16[3584,1024]{1,0:T(8,128)(2,1)} %bitcast.11, bf16[1024,3584]{1,0:T(8,128)(2,1)} %bitcast.13), custom_call_target="tpu_custom_call" | custom-call | flops 18790481920 | bytes 47710208 | tf_op jit(solution)/shard_map/expert/pallas_call | solution.py:125
  146.6 18.6 %all-to-all-done.2.in_ref = bf16[128,4,3584]{2,1,0:T(4,128)(2,1)} async-done(((bf16[128,4,3584]{2,1,0:T(4,128)(2,1)}), bf16[128,4,3584]{2,1,0:T(4,128)(2,1)}, u32[]{:S(2)}, u32[]{:S(2)}) %all-to-all-start.2) | async-done | bytes 3670048 | tf_op jit(solution)/shard_map/all_to_all | solution.py:235
  165.2 4.8 %all-to-all-start.1 = ((bf16[128,4,3584]{2,1,0:T(4,128)(2,1)}), bf16[128,4,3584]{2,1,0:T(4,128)(2,1)}, u32[]{:S(2)}, u32[]{:S(2)}) async-start(bf16[128,4,3584]{2,1,0:T(4,128)(2,1)} %expert.2), calls=%async_computation.1 | async-start | bytes 7340032 | tf_op jit(solution)/shard_map/all_to_all | solution.py:235
  170.1 22.2 %expert.3 = bf16[128,2,3584]{2,1,0:T(2,128)(2,1)} custom-call(bf16[128,4,3584]{2,1,0:T(4,128)(2,1)} %all-to-all-done.2.in_ref, bf16[3584,1024]{1,0:T(8,128)(2,1)} %bitcast.10, bf16[3584,1024]{1,0:T(8,128)(2,1)} %bitcast.12, bf16[1024,3584]{1,0:T(8,128)(2,1)} %bitcast.14), custom_call_target="tpu_custom_call" | custom-call | flops 9395240960 | bytes 42205184 | tf_op jit(solution)/shard_map/expert/pallas_call | solution.py:125
  192.2 25.3 %all-to-all-done.1.block_ref = bf16[128,4,3584]{2,1,0:T(4,128)(2,1)} async-done(((bf16[128,4,3584]{2,1,0:T(4,128)(2,1)}), bf16[128,4,3584]{2,1,0:T(4,128)(2,1)}, u32[]{:S(2)}, u32[]{:S(2)}) %all-to-all-start.1) | async-done | bytes 3670048 | tf_op jit(solution)/shard_map/all_to_all | solution.py:235
  217.5 3.8 %all-to-all-start.3 = ((bf16[128,2,3584]{2,1,0:T(2,128)(2,1)}), bf16[128,2,3584]{2,1,0:T(2,128)(2,1)S(1)}, u32[]{:S(2)}, u32[]{:S(2)}) async-start(bf16[128,2,3584]{2,1,0:T(2,128)(2,1)} %expert.3), calls=%async_computation.3 | async-start | bytes 3670016 | tf_op jit(solution)/shard_map/all_to_all | solution.py:235
  221.3 5.3 %combine_first.1 = (f32[128,3584]{1,0:T(8,128)}, bf16[256,256]{1,0:T(8,128)(2,1)}) custom-call(s32[3,128]{1,0:T(4,128)} %bitcast.7, f32[3,128]{1,0:T(4,128)} %bitcast.8, bf16[128,4,3584]{2,1,0:T(4,128)(2,1)} %all-to-all-done.1.block_ref), custom_call_target="tpu_custom_call" | custom-call | tf_op jit(solution)/shard_map/combine_first/pallas_call | solution.py:190
  226.7 22.7 %all-to-all-done.3.block_ref = bf16[128,2,3584]{2,1,0:T(2,128)(2,1)S(1)} async-done(((bf16[128,2,3584]{2,1,0:T(2,128)(2,1)}), bf16[128,2,3584]{2,1,0:T(2,128)(2,1)S(1)}, u32[]{:S(2)}, u32[]{:S(2)}) %all-to-all-start.3) | async-done | bytes 1835040 | tf_op jit(solution)/shard_map/all_to_all | solution.py:235
  249.4 2.9 %combine_last.1 = bf16[128,3584]{1,0:T(8,128)(2,1)} custom-call(bf16[256,256]{1,0:T(8,128)(2,1)} %get-tuple-element.10.scale_ref, bf16[128,2,3584]{2,1,0:T(2,128)(2,1)S(1)} %all-to-all-done.3.block_ref, f32[128,3584]{1,0:T(8,128)} %get-tuple-element.12.prior_ref), custom_call_target="tpu_custom_call" | custom-call | tf_op jit(solution)/shard_map/combine_last/pallas_call | solution.py:219
Async XLA Ops:
  5.6 100.9 %all-to-all-start = ((bf16[128,8,3584]{2,1,0:T(8,128)(2,1)}), bf16[128,8,3584]{2,1,0:T(8,128)(2,1)}, u32[]{:S(2)}, u32[]{:S(2)}) async-start(bf16[128,8,3584]{2,1,0:T(8,128)(2,1)} %pack.2), calls=%async_computation | async-start | bytes 14680064 | tf_op jit(solution)/shard_map/all_to_all | solution.py:235
  106.5 58.7 %all-to-all-start.2 = ((bf16[128,4,3584]{2,1,0:T(4,128)(2,1)}), bf16[128,4,3584]{2,1,0:T(4,128)(2,1)}, u32[]{:S(2)}, u32[]{:S(2)}) async-start(bf16[128,4,3584]{2,1,0:T(4,128)(2,1)} %pack.3), calls=%async_computation.2 | async-start | bytes 7340032 | tf_op jit(solution)/shard_map/all_to_all | solution.py:235
  165.2 52.3 %all-to-all-start.1 = ((bf16[128,4,3584]{2,1,0:T(4,128)(2,1)}), bf16[128,4,3584]{2,1,0:T(4,128)(2,1)}, u32[]{:S(2)}, u32[]{:S(2)}) async-start(bf16[128,4,3584]{2,1,0:T(4,128)(2,1)} %expert.2), calls=%async_computation.1 | async-start | bytes 7340032 | tf_op jit(solution)/shard_map/all_to_all | solution.py:235
  217.5 31.9 %all-to-all-start.3 = ((bf16[128,2,3584]{2,1,0:T(2,128)(2,1)}), bf16[128,2,3584]{2,1,0:T(2,128)(2,1)S(1)}, u32[]{:S(2)}, u32[]{:S(2)}) async-start(bf16[128,2,3584]{2,1,0:T(2,128)(2,1)} %expert.3), calls=%async_computation.3 | async-start | bytes 3670016 | tf_op jit(solution)/shard_map/all_to_all | solution.py:235

commit v2 on v1

--- a/solution.py
+++ b/solution.py
@@ -5,9 +5,12 @@
 from jax import lax
 from jax.experimental import pallas as pl
 from jax.experimental.pallas import tpu as pltpu
+from jax.sharding import Mesh
 from jax.sharding import PartitionSpec as P
 
-AXES = ("node", "local")
+CHIPS = (("x", 4), ("y", 4), ("core", 2), ("z", 4))
+OWNERS = ("x", "y", "core", "z")
+PEERS = ("y", "core", "z", "x")
 CHUNKS = ((0, 4), (4, 2))
 VMEM_LIMIT = 60 * 1024 * 1024
 ACROSS = (((1,), (1,)), ((), ()))
@@ -17,9 +20,22 @@
     return pltpu.CompilerParams(dimension_semantics=("arbitrary",), vmem_limit_bytes=VMEM_LIMIT)
 
 
+def peer_experts(experts, tok_rows):
+    sizes = dict(CHIPS)
+    rank = lax.broadcasted_iota(jnp.int32, (experts, tok_rows), 0)
+    place = {}
+    for axis in reversed(PEERS):
+        place[axis] = rank % sizes[axis]
+        rank = rank // sizes[axis]
+    number = jnp.zeros((experts, tok_rows), jnp.int32)
+    for axis in OWNERS:
+        number = number * sizes[axis] + place[axis]
+    return number
+
+
 def slots_of(ids_ref, experts):
     topk, tok_rows = ids_ref.shape
-    numbers = lax.broadcasted_iota(jnp.int32, (experts, tok_rows), 0)
+    numbers = peer_experts(experts, tok_rows)
     member = ids_ref[0:1, :] == numbers
     for k in range(1, topk):
         member = member | (ids_ref[k : k + 1, :] == numbers)
@@ -172,7 +188,7 @@
     @pl.when(pl.program_id(0) == 0)
     def _():
         slot = slots_of(ids_ref, experts)
-        numbers = lax.broadcasted_iota(jnp.int32, (experts, tok_rows), 0)
+        numbers = peer_experts(experts, tok_rows)
         weight = jnp.zeros((experts, tok_rows), jnp.float32)
         for k in range(topk):
             weight = jnp.where(ids_ref[k : k + 1, :] == numbers, gates_ref[k : k + 1, :], weight)
@@ -232,11 +248,11 @@
 
 
 def exchange(block):
-    return lax.all_to_all(block, AXES, split_axis=0, concat_axis=0, tiled=True)
+    return lax.all_to_all(block, PEERS, split_axis=0, concat_axis=0, tiled=True)
 
 
 def body(tokens_in, grad_out, expert_ids, gate_weights, w_gate, w_up, w_down):
-    experts = lax.axis_size("node") * lax.axis_size("local")
+    experts = lax.axis_size(PEERS)
     ids = expert_ids.T
     gates = gate_weights.T
     (first_a, count_a), (first_b, count_b) = CHUNKS
@@ -255,7 +271,9 @@
 
 
 def solution(mesh):
-    rows = P(AXES, None)
-    cube = P(AXES, None, None)
+    sizes = tuple(size for _, size in CHIPS)
+    chips = Mesh(mesh.devices.reshape(sizes), OWNERS)
+    rows = P(OWNERS, None)
+    cube = P(OWNERS, None, None)
     in_specs = (rows, rows, rows, rows, cube, cube, cube)
-    return jax.shard_map(body, mesh=mesh, in_specs=in_specs, out_specs=rows, check_vma=False)
+    return jax.shard_map(body, mesh=chips, in_specs=in_specs, out_specs=rows, check_vma=False)

time: 253 us -> 248 us (0.980)
  waiting for transfers between devices: 152 us -> 144 us
    all_to_all x4, waiting for transfers between devices: 152 us -> 144 us  [exchange(): return lax.all_to_all(block, PEERS, split_axis=0, concat_axis=0, tiled=True)]
where the time goes in v2:
time: 248 us; the launch traced here: 247 us
  waiting for transfers between devices  144 us (58%)
  Pallas kernels  68.8 us (28%)
  starting transfers between devices  33.8 us (14%)
    all_to_all x4, waiting for transfers between devices, exchange(): return lax.all_to_all(block, PEERS, split_axis=0, concat_axis=0, tiled=True)  144 us
    pallas_call x2, Pallas kernels, expert(): pl.pallas_call(functools.partial(expert_body, steps=steps), grid=(2 * ste...  50.8 us
    all_to_all x4, starting transfers between devices, exchange(): return lax.all_to_all(block, PEERS, split_axis=0, concat_axis=0, tiled=True)  33.8 us
    pallas_call x2, Pallas kernels, pack(): pl.pallas_call(functools.partial(pack_body, first=first, count=count, exp...  9.77 us
    pallas_call x1, Pallas kernels, combine_a(): pl.pallas_call(functools.partial(combine_a_body, chunks=chunks, experts=e...  5.36 us
  transfers between devices with their start and end apart: 4, of which 4 were waited for; matrix products, arithmetic and copies ran while one was open for 0% of the time, Pallas kernels for 24%

profile of v2, /device:TPU:1, one launch (start us, length us, event | category | flops | bytes accessed | tf_op | source)
XLA Modules:
  0.0 246.7 jit_solution(17883530659953833746)
XLA Ops:
  0.0 5.6 %pack.2 = bf16[128,8,3584]{2,1,0:T(8,128)(2,1)} custom-call(s32[3,128]{1,0:T(4,128)} %bitcast.5, bf16[128,3584]{1,0:T(8,128)(2,1)} %x_ref.3, bf16[128,3584]{1,0:T(8,128)(2,1)} %y_ref.3), custom_call_target="tpu_custom_call" | custom-call | tf_op jit(solution)/shard_map/pack/pallas_call | solution.py:75
  5.6 11.9 %all-to-all-start = ((bf16[128,8,3584]{2,1,0:T(8,128)(2,1)}), bf16[128,8,3584]{2,1,0:T(8,128)(2,1)}, u32[]{:S(2)}, u32[]{:S(2)}) async-start(bf16[128,8,3584]{2,1,0:T(8,128)(2,1)} %pack.2), calls=%async_computation | async-start | bytes 14680064 | tf_op jit(solution)/shard_map/all_to_all | solution.py:251
  17.5 4.1 %pack.3 = bf16[128,4,3584]{2,1,0:T(4,128)(2,1)} custom-call(s32[3,128]{1,0:T(4,128)} %bitcast.6, bf16[128,3584]{1,0:T(8,128)(2,1)} %x_ref.3, bf16[128,3584]{1,0:T(8,128)(2,1)} %y_ref.3), custom_call_target="tpu_custom_call" | custom-call | tf_op jit(solution)/shard_map/pack/pallas_call | solution.py:75
  21.7 81.7 %all-to-all-done.in_ref = bf16[128,8,3584]{2,1,0:T(8,128)(2,1)} async-done(((bf16[128,8,3584]{2,1,0:T(8,128)(2,1)}), bf16[128,8,3584]{2,1,0:T(8,128)(2,1)}, u32[]{:S(2)}, u32[]{:S(2)}) %all-to-all-start) | async-done | bytes 7340064 | tf_op jit(solution)/shard_map/all_to_all | solution.py:251
  103.4 11.9 %all-to-all-start.2 = ((bf16[128,4,3584]{2,1,0:T(4,128)(2,1)}), bf16[128,4,3584]{2,1,0:T(4,128)(2,1)}, u32[]{:S(2)}, u32[]{:S(2)}) async-start(bf16[128,4,3584]{2,1,0:T(4,128)(2,1)} %pack.3), calls=%async_computation.2 | async-start | bytes 7340032 | tf_op jit(solution)/shard_map/all_to_all | solution.py:251
  115.3 28.7 %expert.2 = bf16[128,4,3584]{2,1,0:T(4,128)(2,1)} custom-call(bf16[128,8,3584]{2,1,0:T(8,128)(2,1)} %all-to-all-done.in_ref, bf16[3584,1024]{1,0:T(8,128)(2,1)} %bitcast.9, bf16[3584,1024]{1,0:T(8,128)(2,1)} %bitcast.11, bf16[1024,3584]{1,0:T(8,128)(2,1)} %bitcast.13), custom_call_target="tpu_custom_call" | custom-call | flops 18790481920 | bytes 47710208 | tf_op jit(solution)/shard_map/expert/pallas_call | solution.py:141
  143.9 17.2 %all-to-all-done.2.in_ref = bf16[128,4,3584]{2,1,0:T(4,128)(2,1)} async-done(((bf16[128,4,3584]{2,1,0:T(4,128)(2,1)}), bf16[128,4,3584]{2,1,0:T(4,128)(2,1)}, u32[]{:S(2)}, u32[]{:S(2)}) %all-to-all-start.2) | async-done | bytes 3670048 | tf_op jit(solution)/shard_map/all_to_all | solution.py:251
  161.1 5.2 %all-to-all-start.1 = ((bf16[128,4,3584]{2,1,0:T(4,128)(2,1)}), bf16[128,4,3584]{2,1,0:T(4,128)(2,1)}, u32[]{:S(2)}, u32[]{:S(2)}) async-start(bf16[128,4,3584]{2,1,0:T(4,128)(2,1)} %expert.2), calls=%async_computation.1 | async-start | bytes 7340032 | tf_op jit(solution)/shard_map/all_to_all | solution.py:251
  166.3 22.2 %expert.3 = bf16[128,2,3584]{2,1,0:T(2,128)(2,1)} custom-call(bf16[128,4,3584]{2,1,0:T(4,128)(2,1)} %all-to-all-done.2.in_ref, bf16[3584,1024]{1,0:T(8,128)(2,1)} %bitcast.10, bf16[3584,1024]{1,0:T(8,128)(2,1)} %bitcast.12, bf16[1024,3584]{1,0:T(8,128)(2,1)} %bitcast.14), custom_call_target="tpu_custom_call" | custom-call | flops 9395240960 | bytes 42205184 | tf_op jit(solution)/shard_map/expert/pallas_call | solution.py:141
  188.5 23.7 %all-to-all-done.1.block_ref = bf16[128,4,3584]{2,1,0:T(4,128)(2,1)} async-done(((bf16[128,4,3584]{2,1,0:T(4,128)(2,1)}), bf16[128,4,3584]{2,1,0:T(4,128)(2,1)}, u32[]{:S(2)}, u32[]{:S(2)}) %all-to-all-start.1) | async-done | bytes 3670048 | tf_op jit(solution)/shard_map/all_to_all | solution.py:251
  212.2 4.8 %all-to-all-start.3 = ((bf16[128,2,3584]{2,1,0:T(2,128)(2,1)}), bf16[128,2,3584]{2,1,0:T(2,128)(2,1)S(1)}, u32[]{:S(2)}, u32[]{:S(2)}) async-start(bf16[128,2,3584]{2,1,0:T(2,128)(2,1)} %expert.3), calls=%async_computation.3 | async-start | bytes 3670016 | tf_op jit(solution)/shard_map/all_to_all | solution.py:251
  217.1 5.4 %combine_first.1 = (f32[128,3584]{1,0:T(8,128)}, bf16[256,256]{1,0:T(8,128)(2,1)}) custom-call(s32[3,128]{1,0:T(4,128)} %bitcast.7, f32[3,128]{1,0:T(4,128)} %bitcast.8, bf16[128,4,3584]{2,1,0:T(4,128)(2,1)} %all-to-all-done.1.block_ref), custom_call_target="tpu_custom_call" | custom-call | tf_op jit(solution)/shard_map/combine_first/pallas_call | solution.py:206
  222.4 21.4 %all-to-all-done.3.block_ref = bf16[128,2,3584]{2,1,0:T(2,128)(2,1)S(1)} async-done(((bf16[128,2,3584]{2,1,0:T(2,128)(2,1)}), bf16[128,2,3584]{2,1,0:T(2,128)(2,1)S(1)}, u32[]{:S(2)}, u32[]{:S(2)}) %all-to-all-start.3) | async-done | bytes 1835040 | tf_op jit(solution)/shard_map/all_to_all | solution.py:251
  243.8 2.9 %combine_last.1 = bf16[128,3584]{1,0:T(8,128)(2,1)} custom-call(bf16[256,256]{1,0:T(8,128)(2,1)} %get-tuple-element.10.scale_ref, bf16[128,2,3584]{2,1,0:T(2,128)(2,1)S(1)} %all-to-all-done.3.block_ref, f32[128,3584]{1,0:T(8,128)} %get-tuple-element.12.prior_ref), custom_call_target="tpu_custom_call" | custom-call | tf_op jit(solution)/shard_map/combine_last/pallas_call | solution.py:235
Async XLA Ops:
  5.6 97.7 %all-to-all-start = ((bf16[128,8,3584]{2,1,0:T(8,128)(2,1)}), bf16[128,8,3584]{2,1,0:T(8,128)(2,1)}, u32[]{:S(2)}, u32[]{:S(2)}) async-start(bf16[128,8,3584]{2,1,0:T(8,128)(2,1)} %pack.2), calls=%async_computation | async-start | bytes 14680064 | tf_op jit(solution)/shard_map/all_to_all | solution.py:251
  103.4 57.7 %all-to-all-start.2 = ((bf16[128,4,3584]{2,1,0:T(4,128)(2,1)}), bf16[128,4,3584]{2,1,0:T(4,128)(2,1)}, u32[]{:S(2)}, u32[]{:S(2)}) async-start(bf16[128,4,3584]{2,1,0:T(4,128)(2,1)} %pack.3), calls=%async_computation.2 | async-start | bytes 7340032 | tf_op jit(solution)/shard_map/all_to_all | solution.py:251
  161.1 51.1 %all-to-all-start.1 = ((bf16[128,4,3584]{2,1,0:T(4,128)(2,1)}), bf16[128,4,3584]{2,1,0:T(4,128)(2,1)}, u32[]{:S(2)}, u32[]{:S(2)}) async-start(bf16[128,4,3584]{2,1,0:T(4,128)(2,1)} %expert.2), calls=%async_computation.1 | async-start | bytes 7340032 | tf_op jit(solution)/shard_map/all_to_all | solution.py:251
  212.2 31.6 %all-to-all-start.3 = ((bf16[128,2,3584]{2,1,0:T(2,128)(2,1)}), bf16[128,2,3584]{2,1,0:T(2,128)(2,1)S(1)}, u32[]{:S(2)}, u32[]{:S(2)}) async-start(bf16[128,2,3584]{2,1,0:T(2,128)(2,1)} %expert.3), calls=%async_computation.3 | async-start | bytes 3670016 | tf_op jit(solution)/shard_map/all_to_all | solution.py:251

commit v3 on v2

--- a/solution.py
+++ b/solution.py
@@ -10,7 +10,7 @@
 
 CHIPS = (("x", 4), ("y", 4), ("core", 2), ("z", 4))
 OWNERS = ("x", "y", "core", "z")
-PEERS = ("y", "core", "z", "x")
+PEERS = ("z", "core", "x", "y")
 CHUNKS = ((0, 4), (4, 2))
 VMEM_LIMIT = 60 * 1024 * 1024
 ACROSS = (((1,), (1,)), ((), ()))

time: 248 us -> 244 us (0.984)
  starting transfers between devices: 33.8 us -> 27.9 us
  waiting for transfers between devices: 144 us -> 147 us
    all_to_all x4, starting transfers between devices: 33.8 us -> 27.9 us  [exchange(): return lax.all_to_all(block, PEERS, split_axis=0, concat_axis=0, tiled=True)]
    all_to_all x4, waiting for transfers between devices: 144 us -> 147 us  [exchange(): return lax.all_to_all(block, PEERS, split_axis=0, concat_axis=0, tiled=True)]
  transfers between devices with their start and end apart: 4 -> 4, of which waited for: 4 -> 4; matrix products, arithmetic and copies ran while one was open for 0% -> 0% of each run, Pallas kernels for 24% -> 25%
where the time goes in v3:
time: 244 us; the launch traced here: 243 us
  waiting for transfers between devices  147 us (60%)
  Pallas kernels  68.8 us (28%)
  starting transfers between devices  27.9 us (11%)
    all_to_all x4, waiting for transfers between devices, exchange(): return lax.all_to_all(block, PEERS, split_axis=0, concat_axis=0, tiled=True)  147 us
    pallas_call x2, Pallas kernels, expert(): pl.pallas_call(functools.partial(expert_body, steps=steps), grid=(2 * ste...  50.8 us
    all_to_all x4, starting transfers between devices, exchange(): return lax.all_to_all(block, PEERS, split_axis=0, concat_axis=0, tiled=True)  27.9 us
    pallas_call x2, Pallas kernels, pack(): pl.pallas_call(functools.partial(pack_body, first=first, count=count, exp...  9.77 us
    pallas_call x1, Pallas kernels, combine_a(): pl.pallas_call(functools.partial(combine_a_body, chunks=chunks, experts=e...  5.36 us
  transfers between devices with their start and end apart: 4, of which 4 were waited for; matrix products, arithmetic and copies ran while one was open for 0% of the time, Pallas kernels for 25%

profile of v3, /device:TPU:1, one launch (start us, length us, event | category | flops | bytes accessed | tf_op | source)
XLA Modules:
  0.0 243.4 jit_solution(16306741127000655258)
XLA Ops:
  0.0 5.6 %pack.2 = bf16[128,8,3584]{2,1,0:T(8,128)(2,1)} custom-call(s32[3,128]{1,0:T(4,128)} %bitcast.5, bf16[128,3584]{1,0:T(8,128)(2,1)} %x_ref.3, bf16[128,3584]{1,0:T(8,128)(2,1)} %y_ref.3), custom_call_target="tpu_custom_call" | custom-call | tf_op jit(solution)/shard_map/pack/pallas_call | solution.py:75
  5.6 11.9 %all-to-all-start = ((bf16[128,8,3584]{2,1,0:T(8,128)(2,1)}), bf16[128,8,3584]{2,1,0:T(8,128)(2,1)}, u32[]{:S(2)}, u32[]{:S(2)}) async-start(bf16[128,8,3584]{2,1,0:T(8,128)(2,1)} %pack.2), calls=%async_computation | async-start | bytes 14680064 | tf_op jit(solution)/shard_map/all_to_all | solution.py:251
  17.5 4.1 %pack.3 = bf16[128,4,3584]{2,1,0:T(4,128)(2,1)} custom-call(s32[3,128]{1,0:T(4,128)} %bitcast.6, bf16[128,3584]{1,0:T(8,128)(2,1)} %x_ref.3, bf16[128,3584]{1,0:T(8,128)(2,1)} %y_ref.3), custom_call_target="tpu_custom_call" | custom-call | tf_op jit(solution)/shard_map/pack/pallas_call | solution.py:75
  21.7 82.7 %all-to-all-done.in_ref = bf16[128,8,3584]{2,1,0:T(8,128)(2,1)} async-done(((bf16[128,8,3584]{2,1,0:T(8,128)(2,1)}), bf16[128,8,3584]{2,1,0:T(8,128)(2,1)}, u32[]{:S(2)}, u32[]{:S(2)}) %all-to-all-start) | async-done | bytes 7340064 | tf_op jit(solution)/shard_map/all_to_all | solution.py:251
  104.4 6.8 %all-to-all-start.2 = ((bf16[128,4,3584]{2,1,0:T(4,128)(2,1)}), bf16[128,4,3584]{2,1,0:T(4,128)(2,1)}, u32[]{:S(2)}, u32[]{:S(2)}) async-start(bf16[128,4,3584]{2,1,0:T(4,128)(2,1)} %pack.3), calls=%async_computation.2 | async-start | bytes 7340032 | tf_op jit(solution)/shard_map/all_to_all | solution.py:251
  111.2 28.7 %expert.2 = bf16[128,4,3584]{2,1,0:T(4,128)(2,1)} custom-call(bf16[128,8,3584]{2,1,0:T(8,128)(2,1)} %all-to-all-done.in_ref, bf16[3584,1024]{1,0:T(8,128)(2,1)} %bitcast.9, bf16[3584,1024]{1,0:T(8,128)(2,1)} %bitcast.11, bf16[1024,3584]{1,0:T(8,128)(2,1)} %bitcast.13), custom_call_target="tpu_custom_call" | custom-call | flops 18790481920 | bytes 47710208 | tf_op jit(solution)/shard_map/expert/pallas_call | solution.py:141
  139.9 18.0 %all-to-all-done.2.in_ref = bf16[128,4,3584]{2,1,0:T(4,128)(2,1)} async-done(((bf16[128,4,3584]{2,1,0:T(4,128)(2,1)}), bf16[128,4,3584]{2,1,0:T(4,128)(2,1)}, u32[]{:S(2)}, u32[]{:S(2)}) %all-to-all-start.2) | async-done | bytes 3670048 | tf_op jit(solution)/shard_map/all_to_all | solution.py:251
  157.9 4.9 %all-to-all-start.1 = ((bf16[128,4,3584]{2,1,0:T(4,128)(2,1)}), bf16[128,4,3584]{2,1,0:T(4,128)(2,1)}, u32[]{:S(2)}, u32[]{:S(2)}) async-start(bf16[128,4,3584]{2,1,0:T(4,128)(2,1)} %expert.2), calls=%async_computation.1 | async-start | bytes 7340032 | tf_op jit(solution)/shard_map/all_to_all | solution.py:251
  162.8 22.2 %expert.3 = bf16[128,2,3584]{2,1,0:T(2,128)(2,1)} custom-call(bf16[128,4,3584]{2,1,0:T(4,128)(2,1)} %all-to-all-done.2.in_ref, bf16[3584,1024]{1,0:T(8,128)(2,1)} %bitcast.10, bf16[3584,1024]{1,0:T(8,128)(2,1)} %bitcast.12, bf16[1024,3584]{1,0:T(8,128)(2,1)} %bitcast.14), custom_call_target="tpu_custom_call" | custom-call | flops 9395240960 | bytes 42205184 | tf_op jit(solution)/shard_map/expert/pallas_call | solution.py:141
  184.9 24.4 %all-to-all-done.1.block_ref = bf16[128,4,3584]{2,1,0:T(4,128)(2,1)} async-done(((bf16[128,4,3584]{2,1,0:T(4,128)(2,1)}), bf16[128,4,3584]{2,1,0:T(4,128)(2,1)}, u32[]{:S(2)}, u32[]{:S(2)}) %all-to-all-start.1) | async-done | bytes 3670048 | tf_op jit(solution)/shard_map/all_to_all | solution.py:251
  209.3 4.3 %all-to-all-start.3 = ((bf16[128,2,3584]{2,1,0:T(2,128)(2,1)}), bf16[128,2,3584]{2,1,0:T(2,128)(2,1)S(1)}, u32[]{:S(2)}, u32[]{:S(2)}) async-start(bf16[128,2,3584]{2,1,0:T(2,128)(2,1)} %expert.3), calls=%async_computation.3 | async-start | bytes 3670016 | tf_op jit(solution)/shard_map/all_to_all | solution.py:251
  213.6 5.4 %combine_first.1 = (f32[128,3584]{1,0:T(8,128)}, bf16[256,256]{1,0:T(8,128)(2,1)}) custom-call(s32[3,128]{1,0:T(4,128)} %bitcast.7, f32[3,128]{1,0:T(4,128)} %bitcast.8, bf16[128,4,3584]{2,1,0:T(4,128)(2,1)} %all-to-all-done.1.block_ref), custom_call_target="tpu_custom_call" | custom-call | tf_op jit(solution)/shard_map/combine_first/pallas_call | solution.py:206
  219.0 21.6 %all-to-all-done.3.block_ref = bf16[128,2,3584]{2,1,0:T(2,128)(2,1)S(1)} async-done(((bf16[128,2,3584]{2,1,0:T(2,128)(2,1)}), bf16[128,2,3584]{2,1,0:T(2,128)(2,1)S(1)}, u32[]{:S(2)}, u32[]{:S(2)}) %all-to-all-start.3) | async-done | bytes 1835040 | tf_op jit(solution)/shard_map/all_to_all | solution.py:251
  240.6 2.9 %combine_last.1 = bf16[128,3584]{1,0:T(8,128)(2,1)} custom-call(bf16[256,256]{1,0:T(8,128)(2,1)} %get-tuple-element.10.scale_ref, bf16[128,2,3584]{2,1,0:T(2,128)(2,1)S(1)} %all-to-all-done.3.block_ref, f32[128,3584]{1,0:T(8,128)} %get-tuple-element.12.prior_ref), custom_call_target="tpu_custom_call" | custom-call | tf_op jit(solution)/shard_map/combine_last/pallas_call | solution.py:235
Async XLA Ops:
  5.6 98.8 %all-to-all-start = ((bf16[128,8,3584]{2,1,0:T(8,128)(2,1)}), bf16[128,8,3584]{2,1,0:T(8,128)(2,1)}, u32[]{:S(2)}, u32[]{:S(2)}) async-start(bf16[128,8,3584]{2,1,0:T(8,128)(2,1)} %pack.2), calls=%async_computation | async-start | bytes 14680064 | tf_op jit(solution)/shard_map/all_to_all | solution.py:251
  104.4 53.5 %all-to-all-start.2 = ((bf16[128,4,3584]{2,1,0:T(4,128)(2,1)}), bf16[128,4,3584]{2,1,0:T(4,128)(2,1)}, u32[]{:S(2)}, u32[]{:S(2)}) async-start(bf16[128,4,3584]{2,1,0:T(4,128)(2,1)} %pack.3), calls=%async_computation.2 | async-start | bytes 7340032 | tf_op jit(solution)/shard_map/all_to_all | solution.py:251
  157.9 51.4 %all-to-all-start.1 = ((bf16[128,4,3584]{2,1,0:T(4,128)(2,1)}), bf16[128,4,3584]{2,1,0:T(4,128)(2,1)}, u32[]{:S(2)}, u32[]{:S(2)}) async-start(bf16[128,4,3584]{2,1,0:T(4,128)(2,1)} %expert.2), calls=%async_computation.1 | async-start | bytes 7340032 | tf_op jit(solution)/shard_map/all_to_all | solution.py:251
  209.3 31.3 %all-to-all-start.3 = ((bf16[128,2,3584]{2,1,0:T(2,128)(2,1)}), bf16[128,2,3584]{2,1,0:T(2,128)(2,1)S(1)}, u32[]{:S(2)}, u32[]{:S(2)}) async-start(bf16[128,2,3584]{2,1,0:T(2,128)(2,1)} %expert.3), calls=%async_computation.3 | async-start | bytes 3670016 | tf_op jit(solution)/shard_map/all_to_all | solution.py:251

commit v4 on v3

--- a/solution.py
+++ b/solution.py
@@ -16,8 +16,8 @@
 ACROSS = (((1,), (1,)), ((), ()))
 
 
-def params():
-    return pltpu.CompilerParams(dimension_semantics=("arbitrary",), vmem_limit_bytes=VMEM_LIMIT)
+def params(limit=VMEM_LIMIT):
+    return pltpu.CompilerParams(dimension_semantics=("arbitrary",), vmem_limit_bytes=limit)
 
 
 def peer_experts(experts, tok_rows):
@@ -216,7 +216,7 @@
             jax.ShapeDtypeStruct(late, jnp.bfloat16),
         ],
         scratch_shapes=[pltpu.VMEM((2 * tok_rows, experts * count), jnp.bfloat16)],
-        compiler_params=params(),
+        compiler_params=params(20 * 1024 * 1024),
         name="combine_first",
     )(ids, gates, returned)
 
@@ -242,7 +242,7 @@
         ],
         out_specs=part,
         out_shape=jax.ShapeDtypeStruct((tok_rows, width), jnp.bfloat16),
-        compiler_params=params(),
+        compiler_params=params(20 * 1024 * 1024),
         name="combine_last",
     )(scale, returned, prior)
 

time: 244 us -> 245 us (level)
  local copies, waits for them, and re-layouts: 0 us -> 2.75 us
    unnamed x0 -> x8, local copies, waits for them, and re-layouts: none -> 2.75 us
  transfers between devices with their start and end apart: 4 -> 4, of which waited for: 4 -> 4; matrix products, arithmetic and copies ran while one was open for 0% -> 0% of each run, Pallas kernels for 25% -> 24%
where the time goes in v4:
time: 245 us; the launch traced here: 244 us
  waiting for transfers between devices  146 us (60%)
  Pallas kernels  67 us (27%)
  starting transfers between devices  27.9 us (11%)
  local copies, waits for them, and re-layouts  2.75 us (1%)
    all_to_all x4, waiting for transfers between devices, exchange(): return lax.all_to_all(block, PEERS, split_axis=0, concat_axis=0, tiled=True)  146 us
    pallas_call x2, Pallas kernels, expert(): pl.pallas_call(functools.partial(expert_body, steps=steps), grid=(2 * ste...  50.9 us
    all_to_all x4, starting transfers between devices, exchange(): return lax.all_to_all(block, PEERS, split_axis=0, concat_axis=0, tiled=True)  27.9 us
    pallas_call x2, Pallas kernels, pack(): pl.pallas_call(functools.partial(pack_body, first=first, count=count, exp...  10 us
  transfers between devices with their start and end apart: 4, of which 4 were waited for; matrix products, arithmetic and copies ran while one was open for 0% of the time, Pallas kernels for 24%

profile of v4, /device:TPU:1, one launch (start us, length us, event | category | flops | bytes accessed | tf_op | source)
XLA Modules:
  0.0 244.0 jit_solution(8245434824959040153)
XLA Ops:
  0.0 5.7 %pack.2 = bf16[128,8,3584]{2,1,0:T(8,128)(2,1)} custom-call(s32[3,128]{1,0:T(4,128)} %bitcast.5, bf16[128,3584]{1,0:T(8,128)(2,1)} %x_ref.3, bf16[128,3584]{1,0:T(8,128)(2,1)} %y_ref.3), custom_call_target="tpu_custom_call" | custom-call | tf_op jit(solution)/shard_map/pack/pallas_call | solution.py:75
  5.7 11.9 %all-to-all-start = ((bf16[128,8,3584]{2,1,0:T(8,128)(2,1)}), bf16[128,8,3584]{2,1,0:T(8,128)(2,1)}, u32[]{:S(2)}, u32[]{:S(2)}) async-start(bf16[128,8,3584]{2,1,0:T(8,128)(2,1)} %pack.2), calls=%async_computation | async-start | bytes 14680064 | tf_op jit(solution)/shard_map/all_to_all | solution.py:251
  17.6 4.3 %pack.3 = bf16[128,4,3584]{2,1,0:T(4,128)(2,1)} custom-call(s32[3,128]{1,0:T(4,128)} %bitcast.6, bf16[128,3584]{1,0:T(8,128)(2,1)} %x_ref.3, bf16[128,3584]{1,0:T(8,128)(2,1)} %y_ref.3), custom_call_target="tpu_custom_call" | custom-call | tf_op jit(solution)/shard_map/pack/pallas_call | solution.py:75
  21.9 82.6 %all-to-all-done.in_ref = bf16[128,8,3584]{2,1,0:T(8,128)(2,1)} async-done(((bf16[128,8,3584]{2,1,0:T(8,128)(2,1)}), bf16[128,8,3584]{2,1,0:T(8,128)(2,1)}, u32[]{:S(2)}, u32[]{:S(2)}) %all-to-all-start) | async-done | bytes 7340064 | tf_op jit(solution)/shard_map/all_to_all | solution.py:251
  104.5 6.8 %all-to-all-start.2 = ((bf16[128,4,3584]{2,1,0:T(4,128)(2,1)}), bf16[128,4,3584]{2,1,0:T(4,128)(2,1)}, u32[]{:S(2)}, u32[]{:S(2)}) async-start(bf16[128,4,3584]{2,1,0:T(4,128)(2,1)} %pack.3), calls=%async_computation.2 | async-start | bytes 7340032 | tf_op jit(solution)/shard_map/all_to_all | solution.py:251
  111.3 28.7 %expert.2 = bf16[128,4,3584]{2,1,0:T(4,128)(2,1)} custom-call(bf16[128,8,3584]{2,1,0:T(8,128)(2,1)} %all-to-all-done.in_ref, bf16[3584,1024]{1,0:T(8,128)(2,1)} %bitcast.9, bf16[3584,1024]{1,0:T(8,128)(2,1)} %bitcast.11, bf16[1024,3584]{1,0:T(8,128)(2,1)} %bitcast.13), custom_call_target="tpu_custom_call" | custom-call | flops 18790481920 | bytes 47710208 | tf_op jit(solution)/shard_map/expert/pallas_call | solution.py:141
  140.0 18.0 %all-to-all-done.2.in_ref = bf16[128,4,3584]{2,1,0:T(4,128)(2,1)} async-done(((bf16[128,4,3584]{2,1,0:T(4,128)(2,1)}), bf16[128,4,3584]{2,1,0:T(4,128)(2,1)}, u32[]{:S(2)}, u32[]{:S(2)}) %all-to-all-start.2) | async-done | bytes 3670048 | tf_op jit(solution)/shard_map/all_to_all | solution.py:251
  158.0 4.9 %all-to-all-start.1 = ((bf16[128,4,3584]{2,1,0:T(4,128)(2,1)}), bf16[128,4,3584]{2,1,0:T(4,128)(2,1)}, u32[]{:S(2)}, u32[]{:S(2)}) async-start(bf16[128,4,3584]{2,1,0:T(4,128)(2,1)} %expert.2), calls=%async_computation.1 | async-start | bytes 7340032 | tf_op jit(solution)/shard_map/all_to_all | solution.py:251
  162.9 22.2 %expert.3 = bf16[128,2,3584]{2,1,0:T(2,128)(2,1)} custom-call(bf16[128,4,3584]{2,1,0:T(4,128)(2,1)} %all-to-all-done.2.in_ref, bf16[3584,1024]{1,0:T(8,128)(2,1)} %bitcast.10, bf16[3584,1024]{1,0:T(8,128)(2,1)} %bitcast.12, bf16[1024,3584]{1,0:T(8,128)(2,1)} %bitcast.14), custom_call_target="tpu_custom_call" | custom-call | flops 9395240960 | bytes 42205184 | tf_op jit(solution)/shard_map/expert/pallas_call | solution.py:141
  185.1 0.0 copy-start.2
  185.1 0.0 copy-start.3
  185.1 24.3 %all-to-all-done.1.block_ref = bf16[128,4,3584]{2,1,0:T(4,128)(2,1)} async-done(((bf16[128,4,3584]{2,1,0:T(4,128)(2,1)}), bf16[128,4,3584]{2,1,0:T(4,128)(2,1)}, u32[]{:S(2)}, u32[]{:S(2)}) %all-to-all-start.1) | async-done | bytes 3670048 | tf_op jit(solution)/shard_map/all_to_all | solution.py:251
  209.4 4.3 %all-to-all-start.3 = ((bf16[128,2,3584]{2,1,0:T(2,128)(2,1)}), bf16[128,2,3584]{2,1,0:T(2,128)(2,1)S(1)}, u32[]{:S(2)}, u32[]{:S(2)}) async-start(bf16[128,2,3584]{2,1,0:T(2,128)(2,1)} %expert.3), calls=%async_computation.3 | async-start | bytes 3670016 | tf_op jit(solution)/shard_map/all_to_all | solution.py:251
  213.8 0.0 copy-done.2
  213.8 0.0 copy-done.3
  213.8 4.3 %combine_first.1 = (f32[128,3584]{1,0:T(8,128)S(1)}, bf16[256,256]{1,0:T(8,128)(2,1)S(1)}) custom-call(s32[3,128]{1,0:T(4,128)S(1)} %bitcast.7, f32[3,128]{1,0:T(4,128)S(1)} %bitcast.8, bf16[128,4,3584]{2,1,0:T(4,128)(2,1)} %all-to-all-done.1.block_ref), custom_call_target="tpu_custom_call" | custom-call | tf_op jit(solution)/shard_map/combine_first/pallas_call | solution.py:206
  218.1 0.0 copy-start
  218.1 1.2 copy-done
  219.4 21.3 %all-to-all-done.3.block_ref = bf16[128,2,3584]{2,1,0:T(2,128)(2,1)S(1)} async-done(((bf16[128,2,3584]{2,1,0:T(2,128)(2,1)}), bf16[128,2,3584]{2,1,0:T(2,128)(2,1)S(1)}, u32[]{:S(2)}, u32[]{:S(2)}) %all-to-all-start.3) | async-done | bytes 1835040 | tf_op jit(solution)/shard_map/all_to_all | solution.py:251
  240.7 0.0 copy-start.1
  240.7 1.5 copy-done.1
  242.2 1.8 combine_last.1
Async XLA Ops:
  5.7 98.8 %all-to-all-start = ((bf16[128,8,3584]{2,1,0:T(8,128)(2,1)}), bf16[128,8,3584]{2,1,0:T(8,128)(2,1)}, u32[]{:S(2)}, u32[]{:S(2)}) async-start(bf16[128,8,3584]{2,1,0:T(8,128)(2,1)} %pack.2), calls=%async_computation | async-start | bytes 14680064 | tf_op jit(solution)/shard_map/all_to_all | solution.py:251
  104.5 53.5 %all-to-all-start.2 = ((bf16[128,4,3584]{2,1,0:T(4,128)(2,1)}), bf16[128,4,3584]{2,1,0:T(4,128)(2,1)}, u32[]{:S(2)}, u32[]{:S(2)}) async-start(bf16[128,4,3584]{2,1,0:T(4,128)(2,1)} %pack.3), calls=%async_computation.2 | async-start | bytes 7340032 | tf_op jit(solution)/shard_map/all_to_all | solution.py:251
  158.0 51.4 %all-to-all-start.1 = ((bf16[128,4,3584]{2,1,0:T(4,128)(2,1)}), bf16[128,4,3584]{2,1,0:T(4,128)(2,1)}, u32[]{:S(2)}, u32[]{:S(2)}) async-start(bf16[128,4,3584]{2,1,0:T(4,128)(2,1)} %expert.2), calls=%async_computation.1 | async-start | bytes 7340032 | tf_op jit(solution)/shard_map/all_to_all | solution.py:251
  185.1 28.7 %copy-start.2 = (s32[128,3]{0,1:T(4,128)S(1)}, s32[128,3]{0,1:T(4,128)}, u32[]{:S(2)}) copy-start(s32[128,3]{0,1:T(4,128)} %param.9) | copy-start | bytes 4612
  185.1 28.7 %copy-start.3 = (f32[128,3]{0,1:T(4,128)S(1)}, f32[128,3]{0,1:T(4,128)}, u32[]{:S(2)}) copy-start(f32[128,3]{0,1:T(4,128)} %param.10) | copy-start | bytes 4612
  209.4 31.3 %all-to-all-start.3 = ((bf16[128,2,3584]{2,1,0:T(2,128)(2,1)}), bf16[128,2,3584]{2,1,0:T(2,128)(2,1)S(1)}, u32[]{:S(2)}, u32[]{:S(2)}) async-start(bf16[128,2,3584]{2,1,0:T(2,128)(2,1)} %expert.3), calls=%async_computation.3 | async-start | bytes 3670016 | tf_op jit(solution)/shard_map/all_to_all | solution.py:251
  218.1 1.3 copy-start
  240.7 1.5 copy-start.1
